TPU v7x, 32 devices: a whole 2x2x4 slice. The times are simulated.
32 devices in a mesh: dp: 4 (over y, x), tensor: 8 (over z, core).
Axes of the slice: x: 2, y: 2, z: 4, core: 2. Of those that a mesh axis runs over, the one named last changes fastest.
Arguments:
- activations: bfloat16 [1024, 16384], P('dp', 'tensor'), may hold values from -6 to 6
- angles: float32 [14, 8192], P(None, 'tensor'), may hold values from -3.140625 to 3.140625
- clip_bits: int32 [64, 16384], P('dp', 'tensor'), may hold values from 0 to 65535, as said below
- codes: bfloat16 [16384, 10240], P('tensor', 'dp'), may hold values from -127 to 127, as said below
- exponents: int32 [10240], replicated, may hold values from -16 to -13
- cotangent: bfloat16 [1024, 10240], P('dp', 'tensor'), may hold values from -6 to 6
Outputs:
- input_grad: bfloat16 [1024, 16384], P('dp', 'tensor')
- angle_grad: float32 [14, 8192], P(None, 'tensor')
Inputs may be any that keep to these rules, and one draw needn't show every extreme that they name: Bit k (0 to 15) of clip_bits[w, i] is the clip mask of token 16 w + k at feature i; higher bits are zero. `codes`: every entry is a whole number.
All inputs are finite; a program needn't handle non-finite values.
Results may differ from a plain program's by a relative error of at most 0.003.
Values may be sent and summed in bfloat16 or wider, within the bound.
No kernel may reach another device: no remote copies, remote signals or barrier semaphores. Data moves between devices by JAX's collectives and lax.ppermute only.
A program may use at most 128 MiB of HBM per device.

v0:
```python
import jax
import jax.numpy as jnp
from jax import lax
from jax.sharding import PartitionSpec as P


def partner(value, axis, apart):
    mask = 2**apart
    pairs = [(source, source ^ mask) for source in range(lax.axis_size(axis))]
    return lax.ppermute(value, axis, pairs)


def unpack_mask(clip_bits, rows, width):
    shifts = jnp.arange(16, dtype=jnp.int32)
    bits = jnp.bitwise_and(jnp.right_shift(clip_bits[:, None, :], shifts[None, :, None]), 1)
    return bits.reshape(rows, width).astype(jnp.float32)


def section_terms(table, section, first, width):
    half = 1 << section
    index = first + jnp.arange(width, dtype=jnp.int32)
    pair = jnp.right_shift(index, section + 1) * half + jnp.bitwise_and(index, half - 1)
    theta = jnp.take(table[section], pair)
    lower = jnp.bitwise_and(index, half) == 0
    sign = jnp.where(lower, -1.0, 1.0).astype(jnp.float32)
    return (jnp.cos(theta), sign * jnp.sin(theta), sign, pair)


def local_partner(field, section):
    half = 1 << section
    column = jnp.arange(field.shape[1], dtype=jnp.int32)
    lower = jnp.bitwise_and(column, half) == 0
    return jnp.where(lower[None, :], jnp.roll(field, -half, axis=1), jnp.roll(field, half, axis=1))


def scatter_terms(term, pair, half_pairs):
    return jnp.zeros((half_pairs,), jnp.float32).at[pair].add(term)


def body(activations, angles, clip_bits, codes, exponents, cotangent):
    rows, width = activations.shape
    sections = angles.shape[0]
    share = angles.shape[1]
    half_pairs = share * lax.axis_size("tensor")
    local_count = width.bit_length() - 1
    place = lax.axis_index("tensor")
    table = lax.all_gather(angles, "tensor", axis=1, tiled=True)
    scale = jnp.exp2(exponents.astype(jnp.float32))
    full_cot = lax.all_gather(cotangent, "tensor", axis=1, tiled=True)
    weight_piece = (
        lax.all_gather(codes, "dp", axis=1, tiled=True).astype(jnp.float32) * scale[None, :]
    ).astype(jnp.bfloat16)
    projected = lax.dot_general(
        full_cot, weight_piece, (((1,), (1,)), ((), ())), preferred_element_type=jnp.float32
    )
    grad_rot = projected * unpack_mask(clip_bits, rows, width)
    first = place * width
    field = activations.astype(jnp.float32)
    stored = [None] * sections
    for section in range(sections):
        cosine, signed, sign, pair = section_terms(table, section, first, width)
        if section < local_count:
            other = local_partner(field, section)
        else:
            other = partner(field.astype(jnp.bfloat16), "tensor", section - local_count).astype(
                field.dtype
            )
            stored[section] = (field, other)
        field = cosine * field + signed * other
    grad = grad_rot
    terms_list = [None] * sections
    for section in reversed(range(sections)):
        cosine, signed, sign, pair = section_terms(table, section, first, width)
        if section < local_count:
            other = local_partner(field, section)
            grad_other = local_partner(grad, section)
            before = cosine * field - signed * other
        else:
            before, before_other = stored[section]
            other = cosine * before_other - signed * before
            grad_other = partner(grad, "tensor", section - local_count)
        terms_list[section] = scatter_terms(jnp.sum(sign * grad * other, axis=0), pair, half_pairs)
        grad = cosine * grad - signed * grad_other
        field = before
    input_grad = grad.astype(jnp.bfloat16)
    collected = jnp.stack(terms_list)
    partial_total = lax.psum_scatter(collected, "tensor", scatter_dimension=1, tiled=True)
    angle_grad = lax.psum(partial_total, "dp")
    return (input_grad, angle_grad)


def solution(mesh):
    placed = (
        P("dp", "tensor"),
        P(None, "tensor"),
        P("dp", "tensor"),
        P("tensor", "dp"),
        P(),
        P("dp", "tensor"),
    )
    return jax.shard_map(
        body,
        mesh=mesh,
        in_specs=placed,
        out_specs=(P("dp", "tensor"), P(None, "tensor")),
        check_vma=False,
    )
```

profile of v0, /device:TPU:0, one launch (start us, length us, event | category | flops | bytes accessed | tf_op | source)
XLA Modules:
  0.0 975.6 jit_solution(11110099458539859929)
XLA Ops:
  11.8 18.1 %all_gather.9 = f32[14,8192]{1,0:T(8,128)S(1)} all-gather(f32[14,1024]{1,0:T(8,128)S(1)} %copy-done.17), channel_id=1, replica_groups=mesh['dp'=4,'tensor'=8] {'tensor'}, dimensions={1}, use_global_device_ids=true | all-gather | bytes 516096 | tf_op jit(solution)/shard_map/all_gather | solution.py:47
  30.3 11.8 %gather_fusion = f32[2048]{0:T(1024)S(1)} fusion(f32[8192]{0:T(1024)S(1)} %bitcast.61, s32[2048]{0:T(1024)S(1)} %get-tuple-element.217), kind=kCustom, calls=%fused_computation.clone | custom fusion | bytes 24576 | tf_op jit(solution)/shard_map/jit(_take)/gather | solution.py:23
  42.1 11.8 %gather_fusion.1 = f32[2048]{0:T(1024)S(1)} fusion(f32[8192]{0:T(1024)S(1)} %bitcast.60, s32[2048]{0:T(1024)S(1)} %get-tuple-element.230), kind=kCustom, calls=%fused_computation.1.clone | custom fusion | bytes 24576 | tf_op jit(solution)/shard_map/jit(_take)/gather | solution.py:23
  53.9 11.8 %gather_fusion.2 = f32[2048]{0:T(1024)S(1)} fusion(f32[8192]{0:T(1024)S(1)} %bitcast.59, s32[2048]{0:T(1024)S(1)} %get-tuple-element.218), kind=kCustom, calls=%fused_computation.2.clone | custom fusion | bytes 24576 | tf_op jit(solution)/shard_map/jit(_take)/gather | solution.py:23
  65.7 11.8 %gather_fusion.3 = f32[2048]{0:T(1024)S(1)} fusion(f32[8192]{0:T(1024)S(1)} %bitcast.58, s32[2048]{0:T(1024)S(1)} %get-tuple-element.219), kind=kCustom, calls=%fused_computation.3.clone | custom fusion | bytes 24576 | tf_op jit(solution)/shard_map/jit(_take)/gather | solution.py:23
  77.5 11.8 %gather_fusion.4 = f32[2048]{0:T(1024)S(1)} fusion(f32[8192]{0:T(1024)S(1)} %bitcast.57, s32[2048]{0:T(1024)S(1)} %get-tuple-element.220), kind=kCustom, calls=%fused_computation.4.clone | custom fusion | bytes 24576 | tf_op jit(solution)/shard_map/jit(_take)/gather | solution.py:23
  89.3 11.8 %gather_fusion.5 = f32[2048]{0:T(1024)S(1)} fusion(f32[8192]{0:T(1024)S(1)} %bitcast.56, s32[2048]{0:T(1024)S(1)} %get-tuple-element.221), kind=kCustom, calls=%fused_computation.5.clone | custom fusion | bytes 24576 | tf_op jit(solution)/shard_map/jit(_take)/gather | solution.py:23
  101.1 11.8 %gather_fusion.6 = f32[2048]{0:T(1024)S(1)} fusion(f32[8192]{0:T(1024)S(1)} %bitcast.55, s32[2048]{0:T(1024)S(1)} %get-tuple-element.222), kind=kCustom, calls=%fused_computation.6.clone | custom fusion | bytes 24576 | tf_op jit(solution)/shard_map/jit(_take)/gather | solution.py:23
  112.9 11.8 %gather_fusion.7 = f32[2048]{0:T(1024)S(1)} fusion(f32[8192]{0:T(1024)S(1)} %bitcast.54, s32[2048]{0:T(1024)S(1)} %get-tuple-element.223), kind=kCustom, calls=%fused_computation.7.clone | custom fusion | bytes 24576 | tf_op jit(solution)/shard_map/jit(_take)/gather | solution.py:23
  124.7 11.8 %gather_fusion.8 = f32[2048]{0:T(1024)S(1)} fusion(f32[8192]{0:T(1024)S(1)} %bitcast.53, s32[2048]{0:T(1024)S(1)} %get-tuple-element.224), kind=kCustom, calls=%fused_computation.8.clone | custom fusion | bytes 24576 | tf_op jit(solution)/shard_map/jit(_take)/gather | solution.py:23
  136.5 11.8 %gather_fusion.9 = f32[2048]{0:T(1024)S(1)} fusion(f32[8192]{0:T(1024)S(1)} %bitcast.52, s32[2048]{0:T(1024)S(1)} %get-tuple-element.225), kind=kCustom, calls=%fused_computation.9.clone | custom fusion | bytes 24576 | tf_op jit(solution)/shard_map/jit(_take)/gather | solution.py:23
  148.3 11.8 %gather_fusion.10 = f32[2048]{0:T(1024)S(1)} fusion(f32[8192]{0:T(1024)S(1)} %bitcast.51, s32[2048]{0:T(1024)S(1)} %get-tuple-element.226), kind=kCustom, calls=%fused_computation.10.clone | custom fusion | bytes 24576 | tf_op jit(solution)/shard_map/jit(_take)/gather | solution.py:23
  189.1 249.2 %all-gather.3.cloned.1.call-done = bf16[2048,10240]{1,0:T(8,128)(2,1)} async-done(((bf16[2048,2560]{1,0:T(8,128)(2,1)}), bf16[2048,10240]{1,0:T(8,128)(2,1)}) %all-gather.3.cloned.1.call-update) | async-done | bytes 41943056 | tf_op jit(solution)/shard_map/all_gather | solution.py:51
  438.3 20.5 %fusion.3 = f32[256,2048]{0,1:T(8,128)} fusion(bf16[256,10240]{1,0:T(8,128)(2,1)} %all-gather.5.cloned.1.call-done, bf16[2048,10240]{1,0:T(8,128)(2,1)} %all-gather.3.cloned.1.call-done, f32[10240]{0:T(1024)S(1)} %multiply_exponential_fusion, s32[256,2048]{0,1:T(8,128)S(1)} %copy-done.2, s32[256]{0:T(256)S(1)} %shift_right_arithmetic.224), kind=kOutput, calls=%fused_computation.32 | convolution fusion | flops 10802429952 | bytes 51422208 | tf_op jit(solution)/shard_map/dot_general | solution.py:53
  464.3 11.8 %gather_fusion.11 = f32[2048]{0:T(1024)S(1)} fusion(f32[8192]{0:T(1024)S(1)} %bitcast.50, s32[2048]{0:T(1024)S(1)} %get-tuple-element.227), kind=kCustom, calls=%fused_computation.11.clone | custom fusion | bytes 24576 | tf_op jit(solution)/shard_map/jit(_take)/gather | solution.py:23
  476.1 11.8 %gather_fusion.13 = f32[2048]{0:T(1024)S(1)} fusion(f32[8192]{0:T(1024)S(1)} %bitcast.49, s32[2048]{0:T(1024)S(1)} %get-tuple-element.229), kind=kCustom, calls=%fused_computation.13.clone | custom fusion | bytes 24576 | tf_op jit(solution)/shard_map/jit(_take)/gather | solution.py:23
  491.0 61.3 %collective-permute-done = f32[256,2048]{0,1:T(8,128)} collective-permute-done((f32[256,2048]{0,1:T(8,128)}, f32[256,2048]{0,1:T(8,128)}, u32[]{:S(2)}, u32[]{:S(2)}) %collective-permute-start) | collective-permute-done | bytes 2097184 | tf_op jit(solution)/shard_map/ppermute | solution.py:10
  552.4 3.5 multiply_subtract_fusion.12
  556.3 11.8 %gather_fusion.12 = f32[2048]{0:T(1024)S(1)} fusion(f32[8192]{0:T(1024)S(1)} %bitcast.48, s32[2048]{0:T(1024)S(1)} %get-tuple-element.228), kind=kCustom, calls=%fused_computation.12.clone | custom fusion | bytes 24576 | tf_op jit(solution)/shard_map/jit(_take)/gather | solution.py:23
  568.1 3.1 fusion.57
  571.2 3.5 collective-permute-start.5
  574.9 49.2 %collective-permute-done.5 = bf16[256,2048]{0,1:T(8,128)(2,1)S(1)} collective-permute-done((bf16[256,2048]{0,1:T(8,128)(2,1)S(1)}, bf16[256,2048]{0,1:T(8,128)(2,1)S(1)}, u32[]{:S(2)}, u32[]{:S(2)}) %collective-permute-start.5) | collective-permute-done | bytes 1048608 | tf_op jit(solution)/shard_map/ppermute | solution.py:10
  626.8 8.2 multiply_reduce_fusion
  640.0 14.7 %scatter_custom_fusion.13 = f32[8192]{0:T(1024)S(1)} fusion(s32[2048]{0:T(1024)S(1)} %bitcast.90, f32[2048]{0:T(1024)S(1)} %get-tuple-element.7, f32[]{:T(128)} %constant.42.clone.1), kind=kCustom, calls=%fused_computation.177 | custom fusion | flops 2048 | bytes 32772 | tf_op jit(solution)/shard_map/scatter-add | solution.py:37
  654.7 14.7 %scatter_custom_fusion.12 = f32[8192]{0:T(1024)S(1)} fusion(s32[2048]{0:T(1024)S(1)} %bitcast.89, f32[2048]{0:T(1024)S(1)} %get-tuple-element.8, f32[]{:T(128)} %constant.42.clone.1), kind=kCustom, calls=%fused_computation.179 | custom fusion | flops 2048 | bytes 32772 | tf_op jit(solution)/shard_map/scatter-add | solution.py:37
  669.4 14.7 %scatter_custom_fusion.11 = f32[8192]{0:T(1024)S(1)} fusion(s32[2048]{0:T(1024)S(1)} %bitcast.88, f32[2048]{0:T(1024)S(1)} %get-tuple-element.9, f32[]{:T(128)} %constant.42.clone.1), kind=kCustom, calls=%fused_computation.181 | custom fusion | flops 2048 | bytes 32772 | tf_op jit(solution)/shard_map/scatter-add | solution.py:37
  684.2 4.7 multiply_reduce_fusion.1
  689.4 3.9 multiply_reduce_fusion.2
  696.3 3.9 multiply_reduce_fusion.3
  703.2 3.4 multiply_reduce_fusion.4
  709.5 3.2 multiply_reduce_fusion.5
  715.4 3.1 multiply_reduce_fusion.6
  721.4 3.2 multiply_reduce_fusion.7
  742.1 3.2 multiply_reduce_fusion.10
  747.6 14.9 %scatter_custom_fusion.10 = f32[8192]{0:T(1024)S(1)} fusion(s32[2048]{0:T(1024)} %bitcast.83, f32[2048]{0:T(1024)S(1)} %get-tuple-element.13, f32[]{:T(128)} %constant.42.clone.1), kind=kCustom, calls=%fused_computation.183 | custom fusion | flops 2048 | bytes 33280 | tf_op jit(solution)/shard_map/scatter-add | solution.py:37
  762.5 14.9 %scatter_custom_fusion.9 = f32[8192]{0:T(1024)S(1)} fusion(s32[2048]{0:T(1024)} %bitcast.86, f32[2048]{0:T(1024)S(1)} %get-tuple-element.15, f32[]{:T(128)} %constant.42.clone.1), kind=kCustom, calls=%fused_computation.185 | custom fusion | flops 2048 | bytes 33280 | tf_op jit(solution)/shard_map/scatter-add | solution.py:37
  777.3 14.9 %scatter_custom_fusion.8 = f32[8192]{0:T(1024)S(1)} fusion(s32[2048]{0:T(1024)} %bitcast.84, f32[2048]{0:T(1024)S(1)} %get-tuple-element.17, f32[]{:T(128)} %constant.42.clone.1), kind=kCustom, calls=%fused_computation.187 | custom fusion | flops 2048 | bytes 33280 | tf_op jit(solution)/shard_map/scatter-add | solution.py:37
  792.2 14.9 %scatter_custom_fusion.7 = f32[8192]{0:T(1024)S(1)} fusion(s32[2048]{0:T(1024)} %bitcast.87, f32[2048]{0:T(1024)S(1)} %get-tuple-element.19, f32[]{:T(128)} %constant.42.clone.1), kind=kCustom, calls=%fused_computation.189 | custom fusion | flops 2048 | bytes 33280 | tf_op jit(solution)/shard_map/scatter-add | solution.py:37
  807.1 15.1 %scatter_custom_fusion.6 = f32[8192]{0:T(1024)S(1)} fusion(s32[2048]{0:T(1024)} %bitcast.85, f32[2048]{0:T(1024)S(1)} %get-tuple-element.21, f32[]{:T(128)} %constant.42.clone.1), kind=kCustom, calls=%fused_computation.191 | custom fusion | flops 2048 | bytes 33280 | tf_op jit(solution)/shard_map/scatter-add | solution.py:37
  822.2 14.9 %scatter_custom_fusion.5 = f32[8192]{0:T(1024)S(1)} fusion(s32[2048]{0:T(1024)} %bitcast.82, f32[2048]{0:T(1024)S(1)} %get-tuple-element.23, f32[]{:T(128)} %constant.42.clone.1), kind=kCustom, calls=%fused_computation.193 | custom fusion | flops 2048 | bytes 33280 | tf_op jit(solution)/shard_map/scatter-add | solution.py:37
  837.1 14.9 %scatter_custom_fusion.4 = f32[8192]{0:T(1024)S(1)} fusion(s32[2048]{0:T(1024)} %bitcast.80, f32[2048]{0:T(1024)S(1)} %get-tuple-element.25, f32[]{:T(128)} %constant.42.clone.1), kind=kCustom, calls=%fused_computation.195 | custom fusion | flops 2048 | bytes 33280 | tf_op jit(solution)/shard_map/scatter-add | solution.py:37
  851.9 14.9 %scatter_custom_fusion.3 = f32[8192]{0:T(1024)S(1)} fusion(s32[2048]{0:T(1024)} %bitcast.81, f32[2048]{0:T(1024)S(1)} %get-tuple-element.27, f32[]{:T(128)} %constant.42.clone.1), kind=kCustom, calls=%fused_computation.197 | custom fusion | flops 2048 | bytes 33280 | tf_op jit(solution)/shard_map/scatter-add | solution.py:37
  866.8 14.9 %scatter_custom_fusion.2 = f32[8192]{0:T(1024)S(1)} fusion(s32[2048]{0:T(1024)} %bitcast.79, f32[2048]{0:T(1024)S(1)} %get-tuple-element.29, f32[]{:T(128)} %constant.42.clone.1), kind=kCustom, calls=%fused_computation.199 | custom fusion | flops 2048 | bytes 33280 | tf_op jit(solution)/shard_map/scatter-add | solution.py:37
  881.6 14.9 %scatter_custom_fusion.1 = f32[8192]{0:T(1024)S(1)} fusion(s32[2048]{0:T(1024)} %bitcast.78, f32[2048]{0:T(1024)S(1)} %get-tuple-element.31, f32[]{:T(128)} %constant.42.clone.1), kind=kCustom, calls=%fused_computation.201 | custom fusion | flops 2048 | bytes 33280 | tf_op jit(solution)/shard_map/scatter-add | solution.py:37
  896.5 6.4 fusion.56
  902.9 14.9 %scatter_custom_fusion = f32[8192]{0:T(1024)S(1)} fusion(s32[2048]{0:T(1024)} %bitcast.77, f32[2048]{0:T(1024)S(1)} %get-tuple-element.33, f32[]{:T(128)} %constant.42.clone.1), kind=kCustom, calls=%fused_computation.203 | custom fusion | flops 2048 | bytes 33280 | tf_op jit(solution)/shard_map/scatter-add | solution.py:37
  926.3 24.4 %reduce-scatter.2.cloned.1.call-done = f32[14,1024]{1,0:T(8,128)} async-done(((f32[14,8192]{1,0:T(8,128)}), f32[14,1024]{1,0:T(8,128)}) %reduce-scatter.2.cloned.1.call-update) | async-done | bytes 57360 | tf_op jit(solution)/shard_map/reduce_scatter | solution.py:87
  950.7 17.9 %psum.7 = f32[14,1024]{1,0:T(8,128)} all-reduce(f32[14,1024]{1,0:T(8,128)} %reduce-scatter.2.cloned.1.call-done), channel_id=1, replica_groups=mesh['dp'=4,'tensor'=8] {'dp'}, use_global_device_ids=true, to_apply=%region_29.31 | all-reduce | flops 14336 | bytes 114688 | tf_op jit(solution)/shard_map/psum | solution.py:88
  (204 shorter events, 93.2 us)
Async XLA Ops:
  7.2 181.9 %all-gather.5.cloned.1.call-start = ((), (), s32[]{:S(2)}) async-start(), calls=%async_computation.2 | async-start | bytes 5898240 | tf_op jit(solution)/shard_map/all_gather | solution.py:49
  7.9 1.2 copy-start.3
  7.9 430.4 %all-gather.3.cloned.1.call-start = ((), (), s32[]{:S(2)}) async-start(), calls=%async_computation.1 | async-start | bytes 52428800 | tf_op jit(solution)/shard_map/all_gather | solution.py:51
  8.7 1.0 copy-start.4
  8.7 942.0 %reduce-scatter.2.cloned.1.call-start = ((), (), s32[]{:S(2)}) async-start(), calls=%async_computation.3 | async-start | bytes 589824 | tf_op jit(solution)/shard_map/reduce_scatter | solution.py:87
  9.9 1.9 copy-start.17
  160.1 6.8 copy-start.20
  160.2 0.6 copy-start.23
  160.2 3.3 copy-start.18
  160.3 0.6 copy-start.13
  160.3 0.6 copy-start.15
  163.2 0.6 copy-start.5
  163.2 0.6 copy-start.7
  166.5 0.6 copy-start.9
  166.6 0.6 copy-start.11
  187.4 1.7 copy-start.1
  187.4 1.7 copy-start.22
  187.4 250.9 %copy-start.2 = (s32[256,2048]{0,1:T(8,128)S(1)}, s32[256,2048]{0,1:T(8,128)}, u32[]{:S(2)}) copy-start(s32[256,2048]{0,1:T(8,128)} %copy.11) | copy-start | bytes 6291460
  458.9 93.5 %collective-permute-start = (f32[256,2048]{0,1:T(8,128)}, f32[256,2048]{0,1:T(8,128)}, u32[]{:S(2)}, u32[]{:S(2)}) collective-permute-start(f32[256,2048]{0,1:T(8,128)} %fusion.3), channel_id=1, source_target_pairs={{0,4},{1,5},{2,6},{3,7},{4,0},{5,1},{6,2},{7,3},{8,12},{9,13},{10,... | collective-permute-start | bytes 6291464 | tf_op jit(solution)/shard_map/ppermute | solution.py:10
  464.3 23.7 %collective-permute-start.3 = (bf16[256,2048]{0,1:T(8,128)(2,1)}, bf16[256,2048]{0,1:T(8,128)(2,1)S(1)}, u32[]{:S(2)}, u32[]{:S(2)}) collective-permute-start(bf16[256,2048]{0,1:T(8,128)(2,1)} %get-tuple-element.11), channel_id=1, source_target_pairs={{0,1},{1,0},{2,3},{3,2},{4,5},{5,4},{6,7},{7,6},{8,9},{9,8},{10,11... | collective-permute-start | bytes 3145736 | tf_op jit(solution)/shard_map/ppermute | solution.py:10
  489.5 78.6 %collective-permute-start.4 = (bf16[256,2048]{0,1:T(8,128)(2,1)}, bf16[256,2048]{0,1:T(8,128)(2,1)}, u32[]{:S(2)}, u32[]{:S(2)}) collective-permute-start(bf16[256,2048]{0,1:T(8,128)(2,1)} %fusion.182), channel_id=1, source_target_pairs={{0,2},{1,3},{2,0},{3,1},{4,6},{5,7},{6,4},{7,5},{8,10},{9,11},{10,... | collective-permute-start | bytes 3145736 | tf_op jit(solution)/shard_map/ppermute | solution.py:10
  555.8 70.9 %collective-permute-start.1 = (f32[256,2048]{0,1:T(8,128)}, f32[256,2048]{0,1:T(8,128)}, u32[]{:S(2)}, u32[]{:S(2)}) collective-permute-start(f32[256,2048]{0,1:T(8,128)} %multiply_subtract_fusion.12), channel_id=1, source_target_pairs={{0,2},{1,3},{2,0},{3,1},{4,6},{5,7},{6,4},{7,5},{8,10},{9,11},{10,... | collective-permute-start | bytes 6291464 | tf_op jit(solution)/shard_map/ppermute | solution.py:10
  571.2 52.8 %collective-permute-start.5 = (bf16[256,2048]{0,1:T(8,128)(2,1)S(1)}, bf16[256,2048]{0,1:T(8,128)(2,1)S(1)}, u32[]{:S(2)}, u32[]{:S(2)}) collective-permute-start(bf16[256,2048]{0,1:T(8,128)(2,1)S(1)} %fusion.57), channel_id=1, source_target_pairs={{0,4},{1,5},{2,6},{3,7},{4,0},{5,1},{6,2},{7,3},{8,12},{9,13},{10,... | collective-permute-start | bytes 3145736 | tf_op jit(solution)/shard_map/ppermute | solution.py:10
  635.0 49.2 %collective-permute-start.2 = (f32[256,2048]{0,1:T(8,128)}, f32[256,2048]{0,1:T(8,128)}, u32[]{:S(2)}, u32[]{:S(2)}) collective-permute-start(f32[256,2048]{0,1:T(8,128)} %get-tuple-element.10), channel_id=1, source_target_pairs={{0,1},{1,0},{2,3},{3,2},{4,5},{5,4},{6,7},{7,6},{8,9},{9,8},{10,11... | collective-permute-start | bytes 6291464 | tf_op jit(solution)/shard_map/ppermute | solution.py:10
  730.3 0.7 copy-start.10
  730.3 0.7 copy-start.12
  730.3 0.7 copy-start.21
  736.7 0.7 copy-start.6
  736.7 0.7 copy-start.8
  736.7 0.7 copy-start.19
  745.3 151.2 %copy-start.24 = (pred[2048]{0:T(1024)(128)(4,1)S(1)}, pred[2048]{0:T(1024)(128)(4,1)}, u32[]{:S(2)}) copy-start(pred[2048]{0:T(1024)(128)(4,1)} %copy-done.23) | copy-start | bytes 6148
  919.9 2.9 copy-start
  919.9 2.9 copy-start.14
  919.9 2.8 copy-start.16
Sparse Core Ops, SparseCore 0:
  9.6 60.3 all-gather.4
  71.8 366.4 all-gather.2
  920.0 30.6 reduce-scatter.1
where the time goes:
time: 986 us; the launch traced here: 976 us
  waiting for transfers between devices  388 us (39%)
  other arithmetic  315 us (32%)
  local copies, waits for them, and re-layouts  193 us (20%)
  blocking collectives  36.1 us (4%)
  matrix products  20.5 us (2%)
  between operations  15.6 us (2%)
    all_gather x1, waiting for transfers between devices, body(): lax.all_gather(codes, 'dp', axis=1, tiled=True).astype(jnp.float32)  249 us
    scatter-add x14, other arithmetic, scatter_terms(): return jnp.zeros((half_pairs,), jnp.float32).at[pair].add(term)  208 us
    gather x14, local copies, waits for them, and re-layouts, section_terms(): theta = jnp.take(table[section], pair)  165 us
    ppermute x6, waiting for transfers between devices, partner(): return lax.ppermute(value, axis, pairs)  113 us
    reduce_sum x12, other arithmetic, body(): jnp.sum(sign * grad * other, axis=0)  49 us
    reduce_scatter x1, waiting for transfers between devices, body(): lax.psum_scatter(collected, 'tensor', scatter_dimension=1, tiled=True)  24.4 us
    add x10, other arithmetic, body(): field = cosine * field + signed * other  22.2 us
    dot_general x1, matrix products, body(): lax.dot_general(full_cot, weight_piece, (((1,), (1,)), ((), ())), preferr...  20.5 us
  transfers between devices with their start and end apart: 9, of which 5 were waited for; matrix products, arithmetic and copies ran while one was open for 27% of the time, Pallas kernels for 0%

commit v1 on v0

--- a/solution.py
+++ b/solution.py
@@ -1,7 +1,26 @@
+import functools
 import jax
 import jax.numpy as jnp
 from jax import lax
 from jax.sharding import PartitionSpec as P
+
+
+def write_case(q_in, row_axis, at_axis):
+    seen_now = lax.axis_size(row_axis)
+    item_now = lax.axis_index(row_axis)
+    s_next, known = (seen_now, item_now)
+    formed, passed = (q_in, 1)
+    while passed < s_next:
+        z2 = tuple(((i0, i0 ^ passed) for i0 in range(s_next)))
+        carry_in = lax.ppermute(formed, row_axis, z2)
+        main = jnp.concatenate([formed, carry_in], axis=at_axis)
+        k_now = jnp.concatenate([carry_in, formed], axis=at_axis)
+        formed = jnp.where(known & passed == 0, main, k_now)
+        passed = 2 * passed
+    return formed
+
+
+extend_zone = functools.partial(write_case, row_axis="dp", at_axis=1)
 
 
 def partner(value, axis, apart):
@@ -47,9 +66,7 @@
     table = lax.all_gather(angles, "tensor", axis=1, tiled=True)
     scale = jnp.exp2(exponents.astype(jnp.float32))
     full_cot = lax.all_gather(cotangent, "tensor", axis=1, tiled=True)
-    weight_piece = (
-        lax.all_gather(codes, "dp", axis=1, tiled=True).astype(jnp.float32) * scale[None, :]
-    ).astype(jnp.bfloat16)
+    weight_piece = (extend_zone(codes).astype(jnp.float32) * scale[None, :]).astype(jnp.bfloat16)
     projected = lax.dot_general(
         full_cot, weight_piece, (((1,), (1,)), ((), ())), preferred_element_type=jnp.float32
     )

time: 986 us -> 1260 us (1.28)
  waiting for transfers between devices: 388 us -> 634 us
  matrix products: 20.5 us -> 38.8 us
  other arithmetic: 315 us -> 330 us
    ppermute x0 -> x2, waiting for transfers between devices: none -> 494 us  [write_case(): carry_in = lax.ppermute(formed, row_axis, z2)]
    all_gather x1 -> x0, waiting for transfers between devices: 249 us -> none  [body(): lax.all_gather(codes, 'dp', axis=1, tiled=True).astype(jnp.float32)]
    select_n x0 -> x1, other arithmetic: none -> 22.1 us  [write_case(): formed = jnp.where(known & passed == 0, main, k_now)]
    dot_general x1, matrix products: 20.5 us -> 38.8 us  [body(): lax.dot_general(full_cot, weight_piece, (((1,), (1,)), ((), ())), preferr...]
  transfers between devices with their start and end apart: 9 -> 10, of which waited for: 5 -> 6; matrix products, arithmetic and copies ran while one was open for 27% -> 21% of each run, Pallas kernels for 0% -> 0%
where the time goes in v1:
time: 1260 us
  waiting for transfers between devices  634 us (50%)
  other arithmetic  330 us (26%)
  local copies, waits for them, and re-layouts  192 us (15%)
  matrix products  38.8 us (3%)
  blocking collectives  34.2 us (3%)
  between operations  16.1 us (1%)
  starting transfers between devices  12.9 us (1%)
    ppermute x2, waiting for transfers between devices, write_case(): carry_in = lax.ppermute(formed, row_axis, z2)  494 us
    scatter-add x14, other arithmetic, scatter_terms(): return jnp.zeros((half_pairs,), jnp.float32).at[pair].add(term)  207 us
    gather x14, local copies, waits for them, and re-layouts, section_terms(): theta = jnp.take(table[section], pair)  165 us
    ppermute x6, waiting for transfers between devices, partner(): return lax.ppermute(value, axis, pairs)  113 us
    reduce_sum x12, other arithmetic, body(): jnp.sum(sign * grad * other, axis=0)  45.7 us
    dot_general x1, matrix products, body(): lax.dot_general(full_cot, weight_piece, (((1,), (1,)), ((), ())), preferr...  38.8 us
    reduce_scatter x1, waiting for transfers between devices, body(): lax.psum_scatter(collected, 'tensor', scatter_dimension=1, tiled=True)  27.1 us
  transfers between devices with their start and end apart: 10, of which 6 were waited for; matrix products, arithmetic and copies ran while one was open for 21% of the time, Pallas kernels for 0%

profile of v1, /device:TPU:0, one launch (start us, length us, event | category | flops | bytes accessed | tf_op | source)
XLA Modules:
  0.0 1258.3 jit_solution(15353627693217996631)
XLA Ops:
  10.2 225.7 %collective-permute-done = bf16[2048,2560]{1,0:T(8,128)(2,1)} collective-permute-done((bf16[2048,2560]{1,0:T(8,128)(2,1)}, bf16[2048,2560]{1,0:T(8,128)(2,1)}, u32[]{:S(2)}, u32[]{:S(2)}) %collective-permute-start) | collective-permute-done | bytes 10485792 | tf_op jit(solution)/shard_map/ppermute | solution.py:15
  236.0 22.1 %maximum_select_fusion.2 = bf16[2048,5120]{1,0:T(8,128)(2,1)} fusion(bf16[2048,2560]{1,0:T(8,128)(2,1)} %collective-permute-done, bf16[2048,2560]{1,0:T(8,128)(2,1)} %param.11, pred[]{:T(512)S(6)} %eq.251), kind=kLoop, calls=%fused_computation.38 | loop fusion | flops 94371840 | bytes 41943040 | tf_op jit(solution)/shard_map/jit(_where)/select_n | solution.py:18
  260.5 16.2 %all_gather.6 = f32[14,8192]{1,0:T(8,128)S(1)} all-gather(f32[14,1024]{1,0:T(8,128)S(1)} %copy-done.29), channel_id=1, replica_groups=mesh['dp'=4,'tensor'=8] {'tensor'}, dimensions={1}, use_global_device_ids=true | all-gather | bytes 516096 | tf_op jit(solution)/shard_map/all_gather | solution.py:66
  277.7 12.0 gather_fusion
  289.7 11.8 gather_fusion.1
  301.5 11.8 gather_fusion.2
  313.3 11.8 gather_fusion.3
  325.1 11.8 gather_fusion.4
  336.9 11.8 gather_fusion.5
  348.7 11.8 gather_fusion.6
  360.5 11.8 gather_fusion.7
  372.3 11.8 gather_fusion.8
  384.1 11.8 gather_fusion.9
  395.9 11.8 gather_fusion.10
  441.6 268.1 %collective-permute-done.1 = bf16[2048,5120]{1,0:T(8,128)(2,1)} collective-permute-done((bf16[2048,5120]{1,0:T(8,128)(2,1)}, bf16[2048,5120]{1,0:T(8,128)(2,1)}, u32[]{:S(2)}, u32[]{:S(2)}) %collective-permute-start.1) | collective-permute-done | bytes 20971552 | tf_op jit(solution)/shard_map/ppermute | solution.py:15
  709.7 38.8 %fusion.9 = f32[256,2048]{0,1:T(8,128)} fusion(bf16[256,10240]{1,0:T(8,128)(2,1)} %all-gather.2.cloned.1.call-done, bf16[2048,5120]{1,0:T(8,128)(2,1)} %collective-permute-done.1, bf16[2048,5120]{1,0:T(8,128)(2,1)} %maximum_select_fusion.2, f32[10240]{0:T(1024)S(1)} %multiply_exponential_fusion, pred[]{:T(512)S(6)} %eq.250, s32[256,2048]{0,1:T(8,128)S(1)} %copy-done.2, ...), kind=kOutput, calls=%fused_computation.40 | convolution fusion | flops 10991173632 | bytes 51422208 | tf_op jit(solution)/shard_map/dot_general | solution.py:70
  754.1 11.8 gather_fusion.11
  765.9 11.8 gather_fusion.13
  780.9 59.8 %collective-permute-done.2 = f32[256,2048]{0,1:T(8,128)} collective-permute-done((f32[256,2048]{0,1:T(8,128)}, f32[256,2048]{0,1:T(8,128)}, u32[]{:S(2)}, u32[]{:S(2)}) %collective-permute-start.2) | collective-permute-done | bytes 2097184 | tf_op jit(solution)/shard_map/ppermute | solution.py:29
  840.7 3.5 multiply_subtract_fusion.12
  844.5 11.8 gather_fusion.12
  856.4 3.1 fusion.63
  859.5 3.5 collective-permute-start.7
  863.1 49.2 %collective-permute-done.7 = bf16[256,2048]{0,1:T(8,128)(2,1)S(1)} collective-permute-done((bf16[256,2048]{0,1:T(8,128)(2,1)S(1)}, bf16[256,2048]{0,1:T(8,128)(2,1)S(1)}, u32[]{:S(2)}, u32[]{:S(2)}) %collective-permute-start.7) | collective-permute-done | bytes 1048608 | tf_op jit(solution)/shard_map/ppermute | solution.py:29
  912.3 4.5 collective-permute-done.3
  916.7 8.8 multiply_reduce_fusion
  927.6 14.7 %scatter_custom_fusion.12 = f32[8192]{0:T(1024)S(1)} fusion(s32[2048]{0:T(1024)S(1)} %bitcast.90, f32[2048]{0:T(1024)S(1)} %get-tuple-element.8, f32[]{:T(128)} %constant.42.clone.1), kind=kCustom, calls=%fused_computation.187 | custom fusion | flops 2048 | bytes 32772 | tf_op jit(solution)/shard_map/scatter-add | solution.py:56
  942.3 14.7 %scatter_custom_fusion.13 = f32[8192]{0:T(1024)S(1)} fusion(s32[2048]{0:T(1024)S(1)} %bitcast.89, f32[2048]{0:T(1024)S(1)} %get-tuple-element.7, f32[]{:T(128)} %constant.42.clone.1), kind=kCustom, calls=%fused_computation.185 | custom fusion | flops 2048 | bytes 32772 | tf_op jit(solution)/shard_map/scatter-add | solution.py:56
  957.0 15.1 %scatter_custom_fusion.11 = f32[8192]{0:T(1024)S(1)} fusion(s32[2048]{0:T(1024)S(1)} %bitcast.88, f32[2048]{0:T(1024)} %get-tuple-element.9, f32[]{:T(128)} %constant.42.clone.1), kind=kCustom, calls=%fused_computation.189 | custom fusion | flops 2048 | bytes 33280 | tf_op jit(solution)/shard_map/scatter-add | solution.py:56
  972.1 4.6 multiply_reduce_fusion.1
  977.1 4.0 multiply_reduce_fusion.2
  981.7 3.9 multiply_reduce_fusion.3
  988.7 3.4 multiply_reduce_fusion.4
  1027.2 3.2 multiply_reduce_fusion.10
  1034.1 3.2 fusion.62
  1037.3 14.9 %scatter_custom_fusion = f32[8192]{0:T(1024)S(1)} fusion(s32[2048]{0:T(1024)} %bitcast.87, f32[2048]{0:T(1024)S(1)} %get-tuple-element.33, f32[]{:T(128)} %constant.42.clone.1), kind=kCustom, calls=%fused_computation.211 | custom fusion | flops 2048 | bytes 33280 | tf_op jit(solution)/shard_map/scatter-add | solution.py:56
  1052.2 14.7 %scatter_custom_fusion.1 = f32[8192]{0:T(1024)S(1)} fusion(s32[2048]{0:T(1024)S(1)} %bitcast.86, f32[2048]{0:T(1024)S(1)} %get-tuple-element.31, f32[]{:T(128)} %constant.42.clone.1), kind=kCustom, calls=%fused_computation.209 | custom fusion | flops 2048 | bytes 32772 | tf_op jit(solution)/shard_map/scatter-add | solution.py:56
  1066.9 14.7 %scatter_custom_fusion.2 = f32[8192]{0:T(1024)S(1)} fusion(s32[2048]{0:T(1024)S(1)} %bitcast.85, f32[2048]{0:T(1024)S(1)} %get-tuple-element.29, f32[]{:T(128)} %constant.42.clone.1), kind=kCustom, calls=%fused_computation.207 | custom fusion | flops 2048 | bytes 32772 | tf_op jit(solution)/shard_map/scatter-add | solution.py:56
  1081.7 15.0 %scatter_custom_fusion.3 = f32[8192]{0:T(1024)S(1)} fusion(s32[2048]{0:T(1024)S(1)} %bitcast.84, f32[2048]{0:T(1024)S(1)} %get-tuple-element.27, f32[]{:T(128)} %constant.42.clone.1), kind=kCustom, calls=%fused_computation.205 | custom fusion | flops 2048 | bytes 32772 | tf_op jit(solution)/shard_map/scatter-add | solution.py:56
  1096.6 14.7 %scatter_custom_fusion.4 = f32[8192]{0:T(1024)S(1)} fusion(s32[2048]{0:T(1024)S(1)} %bitcast.83, f32[2048]{0:T(1024)S(1)} %get-tuple-element.25, f32[]{:T(128)} %constant.42.clone.1), kind=kCustom, calls=%fused_computation.203 | custom fusion | flops 2048 | bytes 32772 | tf_op jit(solution)/shard_map/scatter-add | solution.py:56
  1111.3 14.7 %scatter_custom_fusion.5 = f32[8192]{0:T(1024)S(1)} fusion(s32[2048]{0:T(1024)S(1)} %bitcast.82, f32[2048]{0:T(1024)S(1)} %get-tuple-element.23, f32[]{:T(128)} %constant.42.clone.1), kind=kCustom, calls=%fused_computation.201 | custom fusion | flops 2048 | bytes 32772 | tf_op jit(solution)/shard_map/scatter-add | solution.py:56
  1126.1 14.7 %scatter_custom_fusion.6 = f32[8192]{0:T(1024)S(1)} fusion(s32[2048]{0:T(1024)S(1)} %bitcast.81, f32[2048]{0:T(1024)S(1)} %get-tuple-element.21, f32[]{:T(128)} %constant.42.clone.1), kind=kCustom, calls=%fused_computation.199 | custom fusion | flops 2048 | bytes 32772 | tf_op jit(solution)/shard_map/scatter-add | solution.py:56
  1140.8 14.7 %scatter_custom_fusion.7 = f32[8192]{0:T(1024)S(1)} fusion(s32[2048]{0:T(1024)S(1)} %bitcast.80, f32[2048]{0:T(1024)S(1)} %get-tuple-element.19, f32[]{:T(128)} %constant.42.clone.1), kind=kCustom, calls=%fused_computation.197 | custom fusion | flops 2048 | bytes 32772 | tf_op jit(solution)/shard_map/scatter-add | solution.py:56
  1155.5 14.7 %scatter_custom_fusion.8 = f32[8192]{0:T(1024)S(1)} fusion(s32[2048]{0:T(1024)S(1)} %bitcast.79, f32[2048]{0:T(1024)S(1)} %get-tuple-element.17, f32[]{:T(128)} %constant.42.clone.1), kind=kCustom, calls=%fused_computation.195 | custom fusion | flops 2048 | bytes 32772 | tf_op jit(solution)/shard_map/scatter-add | solution.py:56
  1170.2 14.7 %scatter_custom_fusion.9 = f32[8192]{0:T(1024)S(1)} fusion(s32[2048]{0:T(1024)S(1)} %bitcast.78, f32[2048]{0:T(1024)S(1)} %get-tuple-element.15, f32[]{:T(128)} %constant.42.clone.1), kind=kCustom, calls=%fused_computation.193 | custom fusion | flops 2048 | bytes 32772 | tf_op jit(solution)/shard_map/scatter-add | solution.py:56
  1185.0 14.7 %scatter_custom_fusion.10 = f32[8192]{0:T(1024)S(1)} fusion(s32[2048]{0:T(1024)S(1)} %bitcast.77, f32[2048]{0:T(1024)S(1)} %get-tuple-element.13, f32[]{:T(128)} %constant.42.clone.1), kind=kCustom, calls=%fused_computation.191 | custom fusion | flops 2048 | bytes 32772 | tf_op jit(solution)/shard_map/scatter-add | solution.py:56
  1206.0 27.1 %reduce-scatter.2.cloned.1.call-done = f32[14,1024]{1,0:T(8,128)} async-done(((f32[14,8192]{1,0:T(8,128)}), f32[14,1024]{1,0:T(8,128)}) %reduce-scatter.2.cloned.1.call-update) | async-done | bytes 57360 | tf_op jit(solution)/shard_map/reduce_scatter | solution.py:104
  1233.0 18.0 %psum.7 = f32[14,1024]{1,0:T(8,128)} all-reduce(f32[14,1024]{1,0:T(8,128)} %reduce-scatter.2.cloned.1.call-done), channel_id=1, replica_groups=mesh['dp'=4,'tensor'=8] {'dp'}, use_global_device_ids=true, to_apply=%region_29.31 | all-reduce | flops 14336 | bytes 114688 | tf_op jit(solution)/shard_map/psum | solution.py:105
  (242 shorter events, 99.7 us)
Async XLA Ops:
  7.2 434.4 %all-gather.2.cloned.1.call-start = ((), (), s32[]{:S(2)}) async-start(), calls=%async_computation.1 | async-start | bytes 5898240 | tf_op jit(solution)/shard_map/all_gather | solution.py:68
  7.2 228.7 %collective-permute-start = (bf16[2048,2560]{1,0:T(8,128)(2,1)}, bf16[2048,2560]{1,0:T(8,128)(2,1)}, u32[]{:S(2)}, u32[]{:S(2)}) collective-permute-start(bf16[2048,2560]{1,0:T(8,128)(2,1)} %param.11), channel_id=1, source_target_pairs={{0,8},{8,0},{16,24},{24,16},{1,9},{9,1},{17,25},{25,17},{2,10},{10... | collective-permute-start | bytes 31457288 | tf_op jit(solution)/shard_map/ppermute | solution.py:15
  10.2 249.7 %copy-start.3 = (bf16[256,2048]{1,0:T(8,128)(2,1)S(1)}, bf16[256,2048]{1,0:T(8,128)(2,1)}, u32[]{:S(2)}) copy-start(bf16[256,2048]{1,0:T(8,128)(2,1)} %param.8) | copy-start | bytes 3145732
  258.0 2.5 copy-start.29
  258.0 451.6 %collective-permute-start.1 = (bf16[2048,5120]{1,0:T(8,128)(2,1)}, bf16[2048,5120]{1,0:T(8,128)(2,1)}, u32[]{:S(2)}, u32[]{:S(2)}) collective-permute-start(bf16[2048,5120]{1,0:T(8,128)(2,1)} %maximum_select_fusion.2), channel_id=1, source_target_pairs={{0,16},{8,24},{16,0},{24,8},{1,17},{9,25},{17,1},{25,9},{2,18},{10... | collective-permute-start | bytes 62914568 | tf_op jit(solution)/shard_map/ppermute | solution.py:15
  259.9 973.1 %reduce-scatter.2.cloned.1.call-start = ((), (), s32[]{:S(2)}) async-start(), calls=%async_computation.2 | async-start | bytes 589824 | tf_op jit(solution)/shard_map/reduce_scatter | solution.py:104
  407.7 3.4 copy-start.30
  407.8 6.3 copy-start.38
  407.8 9.6 copy-start.32
  407.8 16.5 %copy-start.34 = (pred[2048]{0:T(1024)(128)(4,1)}, pred[2048]{0:T(1024)(128)(4,1)S(1)}, u32[]{:S(2)}) copy-start(pred[2048]{0:T(1024)(128)(4,1)S(1)} %get-tuple-element.245) | copy-start | bytes 6148
  407.8 18.9 %copy-start.36 = (pred[2048]{0:T(1024)(128)(4,1)}, pred[2048]{0:T(1024)(128)(4,1)S(1)}, u32[]{:S(2)}) copy-start(pred[2048]{0:T(1024)(128)(4,1)S(1)} %get-tuple-element.246) | copy-start | bytes 6148
  407.9 0.6 copy-start.25
  410.8 0.6 copy-start.17
  416.6 0.8 copy-start.4
  416.6 0.8 copy-start.6
  416.6 7.6 copy-start.9
  416.7 7.6 copy-start.11
  416.7 9.9 copy-start.13
  416.7 9.9 copy-start.15
  417.4 2.0 copy-start.8
  439.9 1.7 copy-start.1
  439.9 1.6 copy-start.40
  439.9 269.8 %copy-start.2 = (s32[256,2048]{0,1:T(8,128)S(1)}, s32[256,2048]{0,1:T(8,128)}, u32[]{:S(2)}) copy-start(s32[256,2048]{0,1:T(8,128)} %copy.11) | copy-start | bytes 6291460
  748.5 92.2 %collective-permute-start.2 = (f32[256,2048]{0,1:T(8,128)}, f32[256,2048]{0,1:T(8,128)}, u32[]{:S(2)}, u32[]{:S(2)}) collective-permute-start(f32[256,2048]{0,1:T(8,128)} %fusion.9), channel_id=1, source_target_pairs={{0,4},{1,5},{2,6},{3,7},{4,0},{5,1},{6,2},{7,3},{8,12},{9,13},{10,... | collective-permute-start | bytes 6291464 | tf_op jit(solution)/shard_map/ppermute | solution.py:29
  754.1 23.7 %collective-permute-start.5 = (bf16[256,2048]{0,1:T(8,128)(2,1)}, bf16[256,2048]{0,1:T(8,128)(2,1)S(1)}, u32[]{:S(2)}, u32[]{:S(2)}) collective-permute-start(bf16[256,2048]{0,1:T(8,128)(2,1)} %get-tuple-element.11), channel_id=1, source_target_pairs={{0,1},{1,0},{2,3},{3,2},{4,5},{5,4},{6,7},{7,6},{8,9},{9,8},{10,11... | collective-permute-start | bytes 3145736 | tf_op jit(solution)/shard_map/ppermute | solution.py:29
  779.3 77.1 %collective-permute-start.6 = (bf16[256,2048]{0,1:T(8,128)(2,1)}, bf16[256,2048]{0,1:T(8,128)(2,1)}, u32[]{:S(2)}, u32[]{:S(2)}) collective-permute-start(bf16[256,2048]{0,1:T(8,128)(2,1)} %fusion.189), channel_id=1, source_target_pairs={{0,2},{1,3},{2,0},{3,1},{4,6},{5,7},{6,4},{7,5},{8,10},{9,11},{10,... | collective-permute-start | bytes 3145736 | tf_op jit(solution)/shard_map/ppermute | solution.py:29
  840.7 3.8 copy-start
  844.2 72.5 %collective-permute-start.3 = (f32[256,2048]{0,1:T(8,128)}, f32[256,2048]{0,1:T(8,128)}, u32[]{:S(2)}, u32[]{:S(2)}) collective-permute-start(f32[256,2048]{0,1:T(8,128)} %multiply_subtract_fusion.12), channel_id=1, source_target_pairs={{0,2},{1,3},{2,0},{3,1},{4,6},{5,7},{6,4},{7,5},{8,10},{9,11},{10,... | collective-permute-start | bytes 6291464 | tf_op jit(solution)/shard_map/ppermute | solution.py:29
  859.5 52.8 %collective-permute-start.7 = (bf16[256,2048]{0,1:T(8,128)(2,1)S(1)}, bf16[256,2048]{0,1:T(8,128)(2,1)S(1)}, u32[]{:S(2)}, u32[]{:S(2)}) collective-permute-start(bf16[256,2048]{0,1:T(8,128)(2,1)S(1)} %fusion.63), channel_id=1, source_target_pairs={{0,4},{1,5},{2,6},{3,7},{4,0},{5,1},{6,2},{7,3},{8,12},{9,13},{10,... | collective-permute-start | bytes 3145736 | tf_op jit(solution)/shard_map/ppermute | solution.py:29
  925.5 46.5 %collective-permute-start.4 = (f32[256,2048]{0,1:T(8,128)}, f32[256,2048]{0,1:T(8,128)}, u32[]{:S(2)}, u32[]{:S(2)}) collective-permute-start(f32[256,2048]{0,1:T(8,128)} %get-tuple-element.10), channel_id=1, source_target_pairs={{0,1},{1,0},{2,3},{3,2},{4,5},{5,4},{6,7},{7,6},{8,9},{9,8},{10,11... | collective-permute-start | bytes 6291464 | tf_op jit(solution)/shard_map/ppermute | solution.py:29
  1000.7 0.7 copy-start.37
  1004.4 0.7 copy-start.14
  1004.4 0.7 copy-start.16
  1007.2 0.7 copy-start.35
  1010.8 0.7 copy-start.10
  1010.8 0.7 copy-start.12
  1013.7 0.7 copy-start.33
  1017.2 0.7 copy-start.5
  1017.2 0.7 copy-start.7
  1019.8 0.7 copy-start.39
  1023.4 0.7 copy-start.22
  1023.4 0.7 copy-start.24
  1026.5 0.7 copy-start.31
  1030.4 0.7 copy-start.18
  1030.4 0.7 copy-start.20
  1033.4 0.7 copy-start.42
  1201.8 0.7 copy-start.26
  1201.8 0.7 copy-start.28
  (5 other events, 3.0 us)
Sparse Core Ops, SparseCore 0:
  260.0 57.4 all-gather.1
  1201.9 31.1 reduce-scatter.1
